TPU v7x, 128 devices: a whole 4x4x4 slice. The times are simulated.
128 devices in a mesh: expert: 4 (over z), seq: 4 (over y), tensor: 8 (over x, core).
Axes of the slice: x: 4, y: 4, z: 4, core: 2. Of those that a mesh axis runs over, the one named last changes fastest.
Arguments:
- tokens: bfloat16 [3072, 7168], P(('expert', 'seq')), may hold values from -6 to 6
- grad_out: bfloat16 [3072, 7168], P(('expert', 'seq')), may hold values from -6 to 6
- expert_ids: int32 [3072, 2], P(('expert', 'seq')), may hold values from 0 to 3, all different within a row; in each aligned block of 192 rows (0 to 191, 192 to 383, ...) at most 128 rows name the same one
- route_weights: bfloat16 [3072, 2], P(('expert', 'seq')), may hold values from 0.099609375 to 1
- gate_weight: bfloat16 [4, 7168, 2048], P('expert', 'seq', 'tensor'), may hold values from -0.0625 to 0.0625
- up_weight: bfloat16 [4, 7168, 2048], P('expert', 'seq', 'tensor'), may hold values from -0.0625 to 0.0625
- down_weight: bfloat16 [4, 7168, 2048], P('expert', 'seq', 'tensor'), may hold values from -0.125 to 0.125
Outputs:
- grad_tokens: bfloat16 [3072, 7168], P(('expert', 'seq'), 'tensor')
- grad_route: float32 [3072, 2], P(('expert', 'seq'))
- grad_gate: float32 [4, 7168, 2048], P('expert', 'seq', 'tensor')
- grad_up: float32 [4, 7168, 2048], P('expert', 'seq', 'tensor')
- grad_down: float32 [4, 7168, 2048], P('expert', 'seq', 'tensor')
Inputs may be any that keep to these rules, and one draw needn't show every extreme that they name: `expert_ids`: the two ids of a row differ. Within each aligned block of 192 rows (the tokens of one group of the expert and seq axes) no expert is named by more than 128 rows, and in some block an expert is named by exactly 128 rows.
All inputs are finite; a program needn't handle non-finite values.
Results may differ from a plain program's by a relative error of at most 0.019.
Values may be sent and summed in bfloat16 or wider, within the bound.
A program may use at most 192 MiB of HBM per device.

v0:
```python
import jax
import jax.numpy as jnp
from jax import lax
from jax.sharding import PartitionSpec as P


def shards(tokens, grad_out, expert_ids, route_weights, gate_weight, up_weight, down_weight):
    expert_count = lax.axis_size("expert")
    seq_count = lax.axis_size("seq")
    tensor_count = lax.axis_size("tensor")
    local_count = gate_weight.shape[0]
    tok_rows = tokens.shape[0]
    model_width = tokens.shape[1]
    part_width = model_width // tensor_count
    per_peer = tok_rows // 6
    peer_count = expert_count * seq_count
    block_rows = local_count * per_peer
    slot_count = peer_count * block_rows
    flat_ids = expert_ids.reshape(-1)
    route_count = flat_ids.shape[0]
    onehot = (
        flat_ids[:, None] == jnp.arange(local_count * expert_count, dtype=jnp.int32)[None, :]
    ).astype(jnp.int32)
    before = jnp.cumsum(onehot, axis=0) - onehot
    ranking = jnp.sum(before * onehot, axis=1)
    local_expert = flat_ids % local_count
    dest_peer = flat_ids // local_count * seq_count + ranking % seq_count
    target = (dest_peer * local_count + local_expert) * per_peer + ranking // seq_count
    source = (
        jnp.full((slot_count,), -1, jnp.int32)
        .at[target]
        .set(jnp.arange(route_count, dtype=jnp.int32))
    )
    filled = source >= 0
    safe_source = jnp.maximum(source, 0)
    token_of = safe_source // 2
    keep = filled[:, None].astype(tokens.dtype)
    weight_send = (
        route_weights.reshape(-1)[safe_source] * filled.astype(route_weights.dtype)
    ).reshape(peer_count, block_rows)
    in_send = (tokens[token_of] * keep).reshape(peer_count, block_rows, model_width)
    out_send = (grad_out[token_of] * keep).reshape(peer_count, block_rows, model_width)
    in_recv, out_recv, weight_recv = (
        lax.all_to_all(in_send, ("expert", "seq"), split_axis=0, concat_axis=0, tiled=True),
        lax.all_to_all(out_send, ("expert", "seq"), split_axis=0, concat_axis=0, tiled=True),
        lax.all_to_all(weight_send, ("expert", "seq"), split_axis=0, concat_axis=0, tiled=True),
    )

    def by_expert(values):
        shaped = values.reshape((peer_count, local_count, per_peer) + values.shape[2:])
        return jnp.swapaxes(shaped, 0, 1).reshape(
            (local_count, peer_count * per_peer) + values.shape[2:]
        )

    def by_peer(values):
        shaped = values.reshape((local_count, peer_count, per_peer) + values.shape[2:])
        return jnp.swapaxes(shaped, 0, 1).reshape((peer_count, block_rows) + values.shape[2:])

    in_rows = by_expert(in_recv)
    out_rows = by_expert(out_recv)
    prob = by_expert(weight_recv).astype(jnp.float32)[:, :, None]
    gate_full, up_full, down_full = (
        lax.all_gather(gate_weight, "seq", axis=1, tiled=True),
        lax.all_gather(up_weight, "seq", axis=1, tiled=True),
        lax.all_gather(down_weight, "seq", axis=1, tiled=True),
    )
    pre_gate = jnp.einsum("emd,edf->emf", in_rows, gate_full, preferred_element_type=jnp.float32)
    pre_up = jnp.einsum("emd,edf->emf", in_rows, up_full, preferred_element_type=jnp.float32)
    sigmoid_gate = jax.nn.sigmoid(pre_gate)
    silu_gate = pre_gate * sigmoid_gate
    hidden = silu_gate * pre_up
    hidden_low = hidden.astype(jnp.bfloat16)
    back_proj = jnp.einsum("emd,edf->emf", out_rows, down_full, preferred_element_type=jnp.float32)
    partial_scores = jnp.sum(hidden * back_proj, axis=2)
    scaled = (prob * out_rows.astype(jnp.float32)).astype(jnp.bfloat16)
    hidden_grad = prob * back_proj
    up_grad = (hidden_grad * silu_gate).astype(jnp.bfloat16)
    gate_grad = (
        hidden_grad * pre_up * sigmoid_gate * (1.0 + pre_gate * (1.0 - sigmoid_gate))
    ).astype(jnp.bfloat16)
    input_terms = jnp.einsum(
        "emf,edf->emd", gate_grad, gate_full, preferred_element_type=jnp.float32
    )
    input_terms = input_terms + jnp.einsum(
        "emf,edf->emd", up_grad, up_full, preferred_element_type=jnp.float32
    )
    route_scores = lax.psum(partial_scores, "tensor")
    input_shards = lax.psum_scatter(
        input_terms.astype(jnp.bfloat16), "tensor", scatter_dimension=2, tiled=True
    ).astype(jnp.float32)
    back_rows, back_scores = (
        lax.all_to_all(
            by_peer(input_shards).astype(jnp.bfloat16),
            ("expert", "seq"),
            split_axis=0,
            concat_axis=0,
            tiled=True,
        ).astype(jnp.float32),
        lax.all_to_all(
            by_peer(route_scores).astype(jnp.bfloat16),
            ("expert", "seq"),
            split_axis=0,
            concat_axis=0,
            tiled=True,
        ).astype(jnp.float32),
    )
    route_rows = back_rows.reshape(slot_count, part_width)[target].reshape(tok_rows, 2, part_width)
    grad_tokens = jnp.sum(route_rows, axis=1).astype(jnp.bfloat16)
    grad_route = back_scores.reshape(slot_count)[target].reshape(tok_rows, 2)
    gate_part = jnp.einsum("emd,emf->edf", in_rows, gate_grad, preferred_element_type=jnp.float32)
    up_part = jnp.einsum("emd,emf->edf", in_rows, up_grad, preferred_element_type=jnp.float32)
    down_part = jnp.einsum("emd,emf->edf", scaled, hidden_low, preferred_element_type=jnp.float32)
    grad_gate, grad_up, grad_down = (
        lax.psum_scatter(
            gate_part.astype(jnp.bfloat16), "seq", scatter_dimension=1, tiled=True
        ).astype(jnp.float32),
        lax.psum_scatter(
            up_part.astype(jnp.bfloat16), "seq", scatter_dimension=1, tiled=True
        ).astype(jnp.float32),
        lax.psum_scatter(
            down_part.astype(jnp.bfloat16), "seq", scatter_dimension=1, tiled=True
        ).astype(jnp.float32),
    )
    return (grad_tokens, grad_route, grad_gate, grad_up, grad_down)


def solution(mesh):
    placed = (
        P(("expert", "seq"), None),
        P(("expert", "seq"), None),
        P(("expert", "seq"), None),
        P(("expert", "seq"), None),
        P("expert", "seq", "tensor"),
        P("expert", "seq", "tensor"),
        P("expert", "seq", "tensor"),
    )
    return jax.shard_map(
        shards,
        mesh=mesh,
        in_specs=placed,
        out_specs=(
            P(("expert", "seq"), "tensor"),
            P(("expert", "seq"), None),
            P("expert", "seq", "tensor"),
            P("expert", "seq", "tensor"),
            P("expert", "seq", "tensor"),
        ),
        check_vma=False,
    )
```

profile of v0, /device:TPU:1, one launch (start us, length us, event | category | flops | bytes accessed | tf_op | source)
XLA Modules:
  0.0 604.9 jit_solution(13995530741329707157)
XLA Ops:
  11.8 2.9 scatter_custom_fusion
  15.7 3.5 gather_fusion
  20.0 8.6 %all-to-all-start = ((bf16[16,1,32]{2,1,0:T(2,128)(2,1)}), bf16[16,1,32]{2,1,0:T(2,128)(2,1)S(1)}, u32[]{:S(2)}, u32[]{:S(2)}) async-start(bf16[16,1,32]{2,1,0:T(2,128)(2,1)} %all_to_all.25), calls=%async_computation | async-start | bytes 16384 | tf_op jit(solution)/shard_map/all_to_all | solution.py:46
  28.7 7.1 %gather_fusion.1 = bf16[512,7168]{1,0:T(8,128)(2,1)} fusion(bf16[192,7168]{1,0:T(8,128)(2,1)S(1)} %copy-done, s32[1024]{0:T(1024)S(1)} %get-tuple-element.29), kind=kCustom, calls=%fused_computation.1 | custom fusion | bytes 14682112 | tf_op jit(solution)/shard_map/gather | solution.py:42
  35.7 15.9 %gather_fusion.2 = bf16[512,7168]{1,0:T(8,128)(2,1)} fusion(bf16[192,7168]{1,0:T(8,128)(2,1)} %param.7, s32[1024]{0:T(1024)S(1)} %get-tuple-element.29), kind=kCustom, calls=%fused_computation.2 | custom fusion | bytes 14682112 | tf_op jit(solution)/shard_map/gather | solution.py:41
  51.6 10.6 %broadcast_multiply_fusion.1 = (bf16[16,32,7168]{2,1,0:T(8,128)(2,1)}, bf16[16,32,7168]{2,1,0:T(8,128)(2,1)}) fusion(bf16[16,32,7168]{2,1,0:T(8,128)(2,1)} %bitcast.67, bf16[16,32]{1,0:T(8,128)(2,1)S(1)} %reshape.301, bf16[16,32,7168]{2,1,0:T(8,128)(2,1)} %bitcast.68), kind=kLoop, calls=%fused_computation.27 | loop fusion | flops 7340032 | bytes 29361152 | tf_op jit(solution)/shard_map/mul | solution.py:42
  62.2 6.7 %all-to-all-start.2 = ((bf16[16,32,7168]{2,1,0:T(8,128)(2,1)}), bf16[16,32,7168]{2,1,0:T(8,128)(2,1)}, u32[]{:S(2)}, u32[]{:S(2)}) async-start(bf16[16,32,7168]{2,1,0:T(8,128)(2,1)} %get-tuple-element.26), calls=%async_computation.2 | async-start | bytes 14680064 | tf_op jit(solution)/shard_map/all_to_all | solution.py:44
  69.7 124.9 %all-to-all-done.2 = bf16[16,32,7168]{2,1,0:T(8,128)(2,1)} async-done(((bf16[16,32,7168]{2,1,0:T(8,128)(2,1)}), bf16[16,32,7168]{2,1,0:T(8,128)(2,1)}, u32[]{:S(2)}, u32[]{:S(2)}) %all-to-all-start.2) | async-done | bytes 7340064 | tf_op jit(solution)/shard_map/all_to_all | solution.py:44
  194.6 4.7 all-to-all-start.1
  200.2 6.2 %fusion.10 = f32[512,256]{0,1:T(8,128)S(1)} fusion(bf16[512,7168]{1,0:T(8,128)(2,1)} %bitcast.5, bf16[1,7168,256]{2,1,0:T(8,128)(2,1)} %all-gather.6.cloned.1.call-done), kind=kOutput, calls=%fused_computation.22 | convolution fusion | flops 1879048192 | bytes 11534336 | tf_op jit(solution)/shard_map/emd,edf->emf/dot_general | solution.py:68
  206.4 6.2 %fusion.7 = f32[512,256]{0,1:T(8,128)S(1)} fusion(bf16[512,7168]{1,0:T(8,128)(2,1)} %bitcast.5, bf16[1,7168,256]{2,1,0:T(8,128)(2,1)} %all-gather.8.cloned.1.call-done), kind=kOutput, calls=%fused_computation.19 | convolution fusion | flops 1879048192 | bytes 11534336 | tf_op jit(solution)/shard_map/emd,edf->emf/dot_general | solution.py:67
  212.7 80.3 %all-gather.4.cloned.1.call-done = bf16[1,7168,256]{2,1,0:T(8,128)(2,1)} async-done(((bf16[1,1792,256]{2,1,0:T(8,128)(2,1)}), bf16[1,7168,256]{2,1,0:T(8,128)(2,1)}) %all-gather.4.cloned.1.call-update) | async-done | bytes 3670032 | tf_op jit(solution)/shard_map/all_gather | solution.py:65
  293.0 30.6 %all-to-all-done.1 = bf16[16,32,7168]{2,1,0:T(8,128)(2,1)} async-done(((bf16[16,32,7168]{2,1,0:T(8,128)(2,1)}), bf16[16,32,7168]{2,1,0:T(8,128)(2,1)}, u32[]{:S(2)}, u32[]{:S(2)}) %all-to-all-start.1) | async-done | bytes 7340064 | tf_op jit(solution)/shard_map/all_to_all | solution.py:45
  323.6 6.6 %multiply_reduce_fusion = (f32[512]{0:T(512)S(1)}, bf16[512,256]{0,1:T(8,128)(2,1)S(1)}, bf16[512,256]{0,1:T(8,128)(2,1)S(1)}) fusion(f32[512,256]{0,1:T(8,128)S(1)} %fusion.10, f32[512,256]{0,1:T(8,128)S(1)} %fusion.7, f32[512]{0:T(512)S(1)} %reshape.300, bf16[512,7168]{1,0:T(8,128)(2,1)} %bitcast.2, bf16[1,7168,256]{2,1,0:T(8,128)(2,1)} %all-gather.4.cloned.1.call-done), kind=kOutput, calls=%fused_computation.30 | convolution fusion | flops 1881275904 | bytes 12587008 | tf_op jit(solution)/shard_map/emd,edf->emf/dot_general | solution.py:73
  330.2 7.3 %fusion.5 = f32[512,7168]{1,0:T(8,128)} fusion(bf16[512,256]{0,1:T(8,128)(2,1)S(1)} %get-tuple-element.23, bf16[1,7168,256]{2,1,0:T(8,128)(2,1)S(1)} %copy-done.3), kind=kOutput, calls=%fused_computation.17 | convolution fusion | flops 1879048192 | bytes 18612224 | tf_op jit(solution)/shard_map/emf,edf->emd/dot_general | solution.py:81
  337.5 10.4 %fusion = bf16[1,512,7168]{2,1,0:T(8,128)(2,1)} fusion(f32[512,7168]{1,0:T(8,128)} %fusion.5, bf16[512,256]{0,1:T(8,128)(2,1)S(1)} %get-tuple-element.24, bf16[1,7168,256]{2,1,0:T(8,128)(2,1)S(1)} %copy-done.2), kind=kOutput, calls=%fused_computation.8 | convolution fusion | flops 1886388224 | bytes 25952256 | tf_op jit(solution)/shard_map/emf,edf->emd/dot_general | solution.py:84
  347.9 31.6 %copy.30 = bf16[1,512,7168]{1,0,2:T(2,128)(2,1)} copy(bf16[1,512,7168]{2,1,0:T(8,128)(2,1)} %fusion) | data formatting | bytes 14680064
  379.5 10.3 %copy.36 = bf16[7168,1,512]{2,0,1:T(8,128)(2,1)} copy(bf16[7168,1,512]{2,1,0:T(2,128)(2,1)} %bitcast.66) | data formatting | bytes 14680064
  390.0 8.0 %fusion.3 = bf16[1,7168,256]{2,1,0:T(8,128)(2,1)} fusion(bf16[512,7168]{1,0:T(8,128)(2,1)} %bitcast.2, f32[512]{0:T(512)S(1)} %reshape.300, f32[512,256]{0,1:T(8,128)S(1)} %fusion.10, f32[512,256]{0,1:T(8,128)S(1)} %fusion.7), kind=kOutput, calls=%fused_computation.14 | convolution fusion | flops 1892679680 | bytes 12060672 | tf_op jit(solution)/shard_map/emd,emf->edf/dot_general | solution.py:112
  398.0 7.7 %fusion.1 = bf16[1,7168,256]{2,1,0:T(8,128)(2,1)} fusion(bf16[512,7168]{1,0:T(8,128)(2,1)} %bitcast.5, bf16[512,256]{0,1:T(8,128)(2,1)S(1)} %get-tuple-element.23), kind=kOutput, calls=%fused_computation.12 | convolution fusion | flops 1880883200 | bytes 11272192 | tf_op jit(solution)/shard_map/emd,emf->edf/dot_general | solution.py:110
  405.7 7.1 %fusion.2 = bf16[1,7168,256]{2,1,0:T(8,128)(2,1)} fusion(bf16[512,7168]{1,0:T(8,128)(2,1)} %bitcast.5, bf16[512,256]{0,1:T(8,128)(2,1)S(1)} %get-tuple-element.24), kind=kOutput, calls=%fused_computation.13 | convolution fusion | flops 1880883200 | bytes 11272192 | tf_op jit(solution)/shard_map/emd,emf->edf/dot_general | solution.py:111
  412.9 23.6 %psum.7 = bf16[1,512]{1,0:T(2,128)(2,1)S(1)} all-reduce(f32[1,512]{1,0:T(1,128)S(1)} %bitcast.71), channel_id=1, replica_groups=mesh['expert'=4,'seq'=4,'tensor'=8] {'tensor'}, use_global_device_ids=true, to_apply=%region_7.8 | all-reduce | flops 512 | bytes 3072 | tf_op jit(solution)/shard_map/psum | solution.py:87
  437.2 3.5 all-to-all-start.4
  442.9 3.3 copy.31
  447.0 6.1 %all-to-all-start.3 = ((bf16[16,32,896]{2,1,0:T(8,128)(2,1)}), bf16[16,32,896]{2,1,0:T(8,128)(2,1)}, u32[]{:S(2)}, u32[]{:S(2)}) async-start(bf16[16,32,896]{2,1,0:T(8,128)(2,1)} %bitcast.9), calls=%async_computation.3 | async-start | bytes 1835008 | tf_op jit(solution)/shard_map/all_to_all | solution.py:92
  453.2 2.8 gather_fusion.4
  456.8 35.1 %reduce-scatter.11.cloned.1.call-done = bf16[1,1792,256]{2,1,0:T(8,128)(2,1)} async-done(((bf16[1,7168,256]{2,1,0:T(8,128)(2,1)}), bf16[1,1792,256]{2,1,0:T(8,128)(2,1)}) %reduce-scatter.11.cloned.1.call-update) | async-done | bytes 917520 | tf_op jit(solution)/shard_map/reduce_scatter | solution.py:120
  494.4 42.0 %reduce-scatter.7.cloned.1.call-done = bf16[1,1792,256]{2,1,0:T(8,128)(2,1)} async-done(((bf16[1,7168,256]{2,1,0:T(8,128)(2,1)}), bf16[1,1792,256]{2,1,0:T(8,128)(2,1)}) %reduce-scatter.7.cloned.1.call-update) | async-done | bytes 917520 | tf_op jit(solution)/shard_map/reduce_scatter | solution.py:114
  539.0 42.1 %reduce-scatter.9.cloned.1.call-done = bf16[1,1792,256]{2,1,0:T(8,128)(2,1)} async-done(((bf16[1,7168,256]{2,1,0:T(8,128)(2,1)}), bf16[1,1792,256]{2,1,0:T(8,128)(2,1)}) %reduce-scatter.9.cloned.1.call-update) | async-done | bytes 917520 | tf_op jit(solution)/shard_map/reduce_scatter | solution.py:117
  586.4 4.7 gather_fusion.3
  591.1 3.0 reshape.298
  594.0 3.7 reduce_sum.33
  (64 shorter events, 23.1 us)
Async XLA Ops:
  7.2 21.5 %copy-start = (bf16[192,7168]{1,0:T(8,128)(2,1)S(1)}, bf16[192,7168]{1,0:T(8,128)(2,1)}, u32[]{:S(2)}) copy-start(bf16[192,7168]{1,0:T(8,128)(2,1)} %param.8) | copy-start | bytes 8257540
  7.2 193.0 %all-gather.6.cloned.1.call-start = ((), (), s32[]{:S(2)}) async-start(), calls=%async_computation.10 | async-start | bytes 4587520 | tf_op jit(solution)/shard_map/all_gather | solution.py:64
  20.0 42.2 %all-to-all-start = ((bf16[16,1,32]{2,1,0:T(2,128)(2,1)}), bf16[16,1,32]{2,1,0:T(2,128)(2,1)S(1)}, u32[]{:S(2)}, u32[]{:S(2)}) async-start(bf16[16,1,32]{2,1,0:T(2,128)(2,1)} %all_to_all.25), calls=%async_computation | async-start | bytes 16384 | tf_op jit(solution)/shard_map/all_to_all | solution.py:46
  62.2 132.4 %all-to-all-start.2 = ((bf16[16,32,7168]{2,1,0:T(8,128)(2,1)}), bf16[16,32,7168]{2,1,0:T(8,128)(2,1)}, u32[]{:S(2)}, u32[]{:S(2)}) async-start(bf16[16,32,7168]{2,1,0:T(8,128)(2,1)} %get-tuple-element.26), calls=%async_computation.2 | async-start | bytes 14680064 | tf_op jit(solution)/shard_map/all_to_all | solution.py:44
  68.9 137.5 %all-gather.8.cloned.1.call-start = ((), (), s32[]{:S(2)}) async-start(), calls=%async_computation.11 | async-start | bytes 4587520 | tf_op jit(solution)/shard_map/all_gather | solution.py:63
  194.6 129.0 %all-to-all-start.1 = ((bf16[16,32,7168]{2,1,0:T(8,128)(2,1)}), bf16[16,32,7168]{2,1,0:T(8,128)(2,1)}, u32[]{:S(2)}, u32[]{:S(2)}) async-start(bf16[16,32,7168]{2,1,0:T(8,128)(2,1)} %get-tuple-element.25), calls=%async_computation.1 | async-start | bytes 14680064 | tf_op jit(solution)/shard_map/all_to_all | solution.py:45
  199.3 93.7 %all-gather.4.cloned.1.call-start = ((), (), s32[]{:S(2)}) async-start(), calls=%async_computation.9 | async-start | bytes 4587520 | tf_op jit(solution)/shard_map/all_gather | solution.py:65
  200.0 240.7 %reduce-scatter.13.cloned.1.call-start = ((), (), s32[]{:S(2)}) async-start(), calls=%async_computation.15 | async-start | bytes 8257536
  323.6 6.6 %copy-start.3 = (bf16[1,7168,256]{2,1,0:T(8,128)(2,1)S(1)}, bf16[1,7168,256]{2,1,0:T(8,128)(2,1)}, u32[]{:S(2)}) copy-start(bf16[1,7168,256]{2,1,0:T(8,128)(2,1)} %all-gather.8.cloned.1.call-done) | copy-start | bytes 11010052
  330.2 7.4 %copy-start.2 = (bf16[1,7168,256]{2,1,0:T(8,128)(2,1)S(1)}, bf16[1,7168,256]{2,1,0:T(8,128)(2,1)}, u32[]{:S(2)}) copy-start(bf16[1,7168,256]{2,1,0:T(8,128)(2,1)} %all-gather.6.cloned.1.call-done) | copy-start | bytes 11010052
  389.9 102.0 %reduce-scatter.11.cloned.1.call-start = ((), (), s32[]{:S(2)}) async-start(), calls=%async_computation.14 | async-start | bytes 4587520 | tf_op jit(solution)/shard_map/reduce_scatter | solution.py:120
  397.9 138.5 %reduce-scatter.7.cloned.1.call-start = ((), (), s32[]{:S(2)}) async-start(), calls=%async_computation.12 | async-start | bytes 4587520 | tf_op jit(solution)/shard_map/reduce_scatter | solution.py:114
  405.7 175.4 %reduce-scatter.9.cloned.1.call-start = ((), (), s32[]{:S(2)}) async-start(), calls=%async_computation.13 | async-start | bytes 4587520 | tf_op jit(solution)/shard_map/reduce_scatter | solution.py:117
  437.2 9.7 %all-to-all-start.4 = ((bf16[16,1,32]{2,1,0:T(2,128)(2,1)}), bf16[16,1,32]{2,1,0:T(2,128)(2,1)S(1)}, u32[]{:S(2)}, u32[]{:S(2)}) async-start(bf16[16,1,32]{2,1,0:T(2,128)(2,1)} %convert_element_type.144), calls=%async_computation.4 | async-start | bytes 16384 | tf_op jit(solution)/shard_map/all_to_all | solution.py:99
  447.0 136.7 %all-to-all-start.3 = ((bf16[16,32,896]{2,1,0:T(8,128)(2,1)}), bf16[16,32,896]{2,1,0:T(8,128)(2,1)}, u32[]{:S(2)}, u32[]{:S(2)}) async-start(bf16[16,32,896]{2,1,0:T(8,128)(2,1)} %bitcast.9), calls=%async_computation.3 | async-start | bytes 1835008 | tf_op jit(solution)/shard_map/all_to_all | solution.py:92
  583.7 14.1 %copy-start.1 = (bf16[192,7168]{1,0:T(8,128)(2,1)S(1)}, bf16[192,7168]{1,0:T(8,128)(2,1)}, u32[]{:S(2)}) copy-start(bf16[192,7168]{1,0:T(8,128)(2,1)} %param.8) | copy-start | bytes 8257540
Sparse Core Ops, SparseCore 0:
  9.7 47.2 all-gather.5
  71.4 91.2 all-gather.7
  201.8 91.1 all-gather.3
  390.0 46.9 reduce-scatter.12
  439.2 52.5 reduce-scatter.10
  494.1 42.2 reduce-scatter.6
  538.8 42.2 reduce-scatter.8
where the time goes:
time: 615 us; the launch traced here: 605 us
  waiting for transfers between devices  358 us (58%)
  local copies, waits for them, and re-layouts  92.3 us (15%)
  matrix products  59.6 us (10%)
  starting transfers between devices  29.8 us (5%)
  other arithmetic  26.9 us (4%)
  blocking collectives  23.6 us (4%)
  between operations  14.6 us (2%)
    all_to_all x1, waiting for transfers between devices, shards(): lax.all_to_all(in_send, ('expert', 'seq'), split_axis=0, concat_axis=0, t...  125 us
    all_gather x1, waiting for transfers between devices, shards(): lax.all_gather(down_weight, 'seq', axis=1, tiled=True)  80.3 us
    unnamed x15, local copies, waits for them, and re-layouts  49.8 us
    reduce_scatter x1, waiting for transfers between devices, shards(): lax.psum_scatter(up_part.astype(jnp.bfloat16), 'seq', scatter_dimension=1...  42.1 us
    reduce_scatter x1, waiting for transfers between devices, shards(): lax.psum_scatter(gate_part.astype(jnp.bfloat16), 'seq', scatter_dimension...  42 us
    reduce_scatter x1, waiting for transfers between devices, shards(): lax.psum_scatter(down_part.astype(jnp.bfloat16), 'seq', scatter_dimension...  35.1 us
    all_to_all x1, waiting for transfers between devices, shards(): lax.all_to_all(out_send, ('expert', 'seq'), split_axis=0, concat_axis=0,...  30.6 us
    psum x1, blocking collectives, shards(): route_scores = lax.psum(partial_scores, 'tensor')  23.6 us
  transfers between devices with their start and end apart: 12, of which 7 were waited for; matrix products, arithmetic and copies ran while one was open for 16% of the time, Pallas kernels for 0%

commit v1 on v0

--- a/solution.py
+++ b/solution.py
@@ -2,6 +2,19 @@
 import jax.numpy as jnp
 from jax import lax
 from jax.sharding import PartitionSpec as P
+
+
+def collect(value, axis, dim):
+    ways = lax.axis_size(axis)
+    up = [(d, (d + 1) % ways) for d in range(ways)]
+    down = [(d, (d - 1) % ways) for d in range(ways)]
+    earlier, later = ([value], [value])
+    for _ in range(ways // 2):
+        earlier.append(lax.ppermute(earlier[-1], axis, up))
+    for _ in range((ways - 1) // 2):
+        later.append(lax.ppermute(later[-1], axis, down))
+    line = jnp.concatenate([*earlier[::-1], *later[1:]], axis=dim)
+    return jnp.roll(line, (lax.axis_index(axis) - ways // 2) * value.shape[dim], axis=dim)
 
 
 def shards(tokens, grad_out, expert_ids, route_weights, gate_weight, up_weight, down_weight):
@@ -62,7 +75,7 @@
     gate_full, up_full, down_full = (
         lax.all_gather(gate_weight, "seq", axis=1, tiled=True),
         lax.all_gather(up_weight, "seq", axis=1, tiled=True),
-        lax.all_gather(down_weight, "seq", axis=1, tiled=True),
+        collect(down_weight, "seq", 1),
     )
     pre_gate = jnp.einsum("emd,edf->emf", in_rows, gate_full, preferred_element_type=jnp.float32)
     pre_up = jnp.einsum("emd,edf->emf", in_rows, up_full, preferred_element_type=jnp.float32)

time: 615 us -> 677 us (1.10)
  waiting for transfers between devices: 358 us -> 394 us
  starting transfers between devices: 29.8 us -> 44 us
  local copies, waits for them, and re-layouts: 92.3 us -> 103 us
    ppermute x0 -> x3, waiting for transfers between devices: none -> 147 us  [the longest x2 147 us: collect(): earlier.append(lax.ppermute(earlier[-1], axis, up))]
    all_gather x1 -> x0, waiting for transfers between devices: 80.3 us -> none  [shards(): lax.all_gather(down_weight, 'seq', axis=1, tiled=True)]
    all_to_all x1, waiting for transfers between devices: 30.6 us -> 0.01 us  [shards(): lax.all_to_all(out_send, ('expert', 'seq'), split_axis=0, concat_axis=0,...]
    ppermute x0 -> x3, starting transfers between devices: none -> 13 us  [the longest x1 7.51 us: collect(): later.append(lax.ppermute(later[-1], axis, down))]
    unnamed x15 -> x24, local copies, waits for them, and re-layouts: 49.8 us -> 59.3 us
    reduce_scatter x1, waiting for transfers between devices: 35.1 us -> 42 us  [shards(): lax.psum_scatter(down_part.astype(jnp.bfloat16), 'seq', scatter_dimension...]
  transfers between devices with their start and end apart: 12 -> 14, of which waited for: 7 -> 7; matrix products, arithmetic and copies ran while one was open for 16% -> 14% of each run, Pallas kernels for 0% -> 0%
where the time goes in v1:
time: 677 us; the launch traced here: 667 us
  waiting for transfers between devices  394 us (58%)
  local copies, waits for them, and re-layouts  103 us (15%)
  matrix products  59 us (9%)
  starting transfers between devices  44 us (6%)
  other arithmetic  26.9 us (4%)
  blocking collectives  25.6 us (4%)
  between operations  14.8 us (2%)
    ppermute x2, waiting for transfers between devices, collect(): earlier.append(lax.ppermute(earlier[-1], axis, up))  147 us
    all_to_all x1, waiting for transfers between devices, shards(): lax.all_to_all(in_send, ('expert', 'seq'), split_axis=0, concat_axis=0, t...  125 us
    unnamed x24, local copies, waits for them, and re-layouts  59.3 us
    reduce_scatter x1, waiting for transfers between devices, shards(): lax.psum_scatter(down_part.astype(jnp.bfloat16), 'seq', scatter_dimension...  42 us
    reduce_scatter x1, waiting for transfers between devices, shards(): lax.psum_scatter(up_part.astype(jnp.bfloat16), 'seq', scatter_dimension=1...  42 us
    reduce_scatter x1, waiting for transfers between devices, shards(): lax.psum_scatter(gate_part.astype(jnp.bfloat16), 'seq', scatter_dimension...  35.7 us
    psum x1, blocking collectives, shards(): route_scores = lax.psum(partial_scores, 'tensor')  25.6 us
    gather x1, local copies, waits for them, and re-layouts, shards(): tokens[token_of] * keep  15.9 us
  transfers between devices with their start and end apart: 14, of which 7 were waited for; matrix products, arithmetic and copies ran while one was open for 14% of the time, Pallas kernels for 0%

profile of v1, /device:TPU:1, one launch (start us, length us, event | category | flops | bytes accessed | tf_op | source)
XLA Modules:
  0.0 666.7 jit_solution(17652051321747972400)
XLA Ops:
  15.1 3.5 gather_fusion
  19.3 8.6 %all-to-all-start = ((bf16[16,1,32]{2,1,0:T(2,128)(2,1)}), bf16[16,1,32]{2,1,0:T(2,128)(2,1)S(1)}, u32[]{:S(2)}, u32[]{:S(2)}) async-start(bf16[16,1,32]{2,1,0:T(2,128)(2,1)} %all_to_all.25), calls=%async_computation | async-start | bytes 16384 | tf_op jit(solution)/shard_map/all_to_all | solution.py:59
  28.0 7.1 %gather_fusion.1 = bf16[512,7168]{1,0:T(8,128)(2,1)} fusion(bf16[192,7168]{1,0:T(8,128)(2,1)S(1)} %copy-done, s32[1024]{0:T(1024)S(1)} %get-tuple-element.29), kind=kCustom, calls=%fused_computation.1 | custom fusion | bytes 14682112 | tf_op jit(solution)/shard_map/gather | solution.py:55
  35.1 15.9 %gather_fusion.2 = bf16[512,7168]{1,0:T(8,128)(2,1)} fusion(bf16[192,7168]{1,0:T(8,128)(2,1)} %param.7, s32[1024]{0:T(1024)S(1)} %get-tuple-element.29), kind=kCustom, calls=%fused_computation.2 | custom fusion | bytes 14682112 | tf_op jit(solution)/shard_map/gather | solution.py:54
  50.9 10.6 %broadcast_multiply_fusion.1 = (bf16[16,32,7168]{2,1,0:T(8,128)(2,1)}, bf16[16,32,7168]{2,1,0:T(8,128)(2,1)}) fusion(bf16[16,32,7168]{2,1,0:T(8,128)(2,1)} %bitcast.67, bf16[16,32]{1,0:T(8,128)(2,1)S(1)} %reshape.301, bf16[16,32,7168]{2,1,0:T(8,128)(2,1)} %bitcast.68), kind=kLoop, calls=%fused_computation.28 | loop fusion | flops 7340032 | bytes 29361152 | tf_op jit(solution)/shard_map/mul | solution.py:55
  61.5 6.7 %all-to-all-start.2 = ((bf16[16,32,7168]{2,1,0:T(8,128)(2,1)}), bf16[16,32,7168]{2,1,0:T(8,128)(2,1)}, u32[]{:S(2)}, u32[]{:S(2)}) async-start(bf16[16,32,7168]{2,1,0:T(8,128)(2,1)} %get-tuple-element.26), calls=%async_computation.2 | async-start | bytes 14680064 | tf_op jit(solution)/shard_map/all_to_all | solution.py:57
  69.0 124.9 %all-to-all-done.2 = bf16[16,32,7168]{2,1,0:T(8,128)(2,1)} async-done(((bf16[16,32,7168]{2,1,0:T(8,128)(2,1)}), bf16[16,32,7168]{2,1,0:T(8,128)(2,1)}, u32[]{:S(2)}, u32[]{:S(2)}) %all-to-all-start.2) | async-done | bytes 7340064 | tf_op jit(solution)/shard_map/all_to_all | solution.py:57
  193.9 4.8 all-to-all-start.1
  200.8 129.2 %collective-permute-done = bf16[1,1792,256]{2,1,0:T(8,128)(2,1)S(1)} collective-permute-done((bf16[1,1792,256]{2,1,0:T(8,128)(2,1)S(1)}, bf16[1,1792,256]{2,1,0:T(8,128)(2,1)S(1)}, u32[]{:S(2)}, u32[]{:S(2)}) %collective-permute-start) | collective-permute-done | bytes 917536 | tf_op jit(solution)/shard_map/ppermute | solution.py:13
  330.0 4.2 collective-permute-start.1
  334.2 7.5 %collective-permute-start.2 = (bf16[1,1792,256]{2,1,0:T(8,128)(2,1)S(1)}, bf16[1,1792,256]{2,1,0:T(8,128)(2,1)S(1)}, u32[]{:S(2)}, u32[]{:S(2)}) collective-permute-start(bf16[1,1792,256]{2,1,0:T(8,128)(2,1)S(1)} %copy-done.3), channel_id=1, source_target_pairs={{0,24},{8,0},{16,8},{24,16},{1,25},{9,1},{17,9},{25,17},{2,26},{10... | collective-permute-start | bytes 2752520 | tf_op jit(solution)/shard_map/ppermute | solution.py:15
  341.8 17.4 %collective-permute-done.1 = bf16[1,1792,256]{2,1,0:T(8,128)(2,1)} collective-permute-done((bf16[1,1792,256]{2,1,0:T(8,128)(2,1)S(1)}, bf16[1,1792,256]{2,1,0:T(8,128)(2,1)}, u32[]{:S(2)}, u32[]{:S(2)}) %collective-permute-start.1) | collective-permute-done | bytes 917536 | tf_op jit(solution)/shard_map/ppermute | solution.py:13
  369.6 6.2 fusion.10
  375.8 6.2 fusion.7
  382.1 6.6 multiply_reduce_fusion
  388.7 7.4 %fusion.5 = f32[512,7168]{1,0:T(8,128)} fusion(bf16[512,256]{0,1:T(8,128)(2,1)S(1)} %get-tuple-element.23, bf16[1,7168,256]{2,1,0:T(8,128)(2,1)S(1)} %copy-done.4), kind=kOutput, calls=%fused_computation.17 | convolution fusion | flops 1879048192 | bytes 18612224 | tf_op jit(solution)/shard_map/emf,edf->emd/dot_general | solution.py:94
  396.1 10.4 %fusion = bf16[1,512,7168]{2,1,0:T(8,128)(2,1)} fusion(f32[512,7168]{1,0:T(8,128)} %fusion.5, bf16[512,256]{0,1:T(8,128)(2,1)S(1)} %get-tuple-element.24, bf16[1,7168,256]{2,1,0:T(8,128)(2,1)S(1)} %copy-done.2), kind=kOutput, calls=%fused_computation.8 | convolution fusion | flops 1886388224 | bytes 25952256 | tf_op jit(solution)/shard_map/emf,edf->emd/dot_general | solution.py:97
  406.5 31.6 %copy.30 = bf16[1,512,7168]{1,0,2:T(2,128)(2,1)} copy(bf16[1,512,7168]{2,1,0:T(8,128)(2,1)} %fusion) | data formatting | bytes 14680064
  438.1 10.3 %copy.36 = bf16[7168,1,512]{2,0,1:T(8,128)(2,1)} copy(bf16[7168,1,512]{2,1,0:T(2,128)(2,1)} %bitcast.66) | data formatting | bytes 14680064
  448.5 7.0 %fusion.1 = bf16[1,7168,256]{2,1,0:T(8,128)(2,1)} fusion(bf16[512,7168]{1,0:T(8,128)(2,1)} %bitcast.5, bf16[512,256]{0,1:T(8,128)(2,1)S(1)} %get-tuple-element.23), kind=kOutput, calls=%fused_computation.12 | convolution fusion | flops 1880883200 | bytes 11272192 | tf_op jit(solution)/shard_map/emd,emf->edf/dot_general | solution.py:123
  455.6 7.1 %fusion.2 = bf16[1,7168,256]{2,1,0:T(8,128)(2,1)} fusion(bf16[512,7168]{1,0:T(8,128)(2,1)} %bitcast.5, bf16[512,256]{0,1:T(8,128)(2,1)S(1)} %get-tuple-element.24), kind=kOutput, calls=%fused_computation.13 | convolution fusion | flops 1880883200 | bytes 11272192 | tf_op jit(solution)/shard_map/emd,emf->edf/dot_general | solution.py:124
  462.7 8.1 %fusion.3 = bf16[1,7168,256]{2,1,0:T(8,128)(2,1)} fusion(bf16[512,7168]{1,0:T(8,128)(2,1)} %bitcast.2, f32[512]{0:T(512)S(1)} %reshape.300, f32[512,256]{0,1:T(8,128)S(1)} %fusion.10, f32[512,256]{0,1:T(8,128)S(1)} %fusion.7), kind=kOutput, calls=%fused_computation.14 | convolution fusion | flops 1892679680 | bytes 12060672 | tf_op jit(solution)/shard_map/emd,emf->edf/dot_general | solution.py:125
  470.9 25.6 %psum.7 = bf16[1,512]{1,0:T(2,128)(2,1)S(1)} all-reduce(f32[1,512]{1,0:T(1,128)S(1)} %bitcast.71), channel_id=1, replica_groups=mesh['expert'=4,'seq'=4,'tensor'=8] {'tensor'}, use_global_device_ids=true, to_apply=%region_7.8 | all-reduce | flops 512 | bytes 3072 | tf_op jit(solution)/shard_map/psum | solution.py:100
  497.2 4.6 all-to-all-start.4
  503.9 3.3 copy.31
  508.1 6.1 all-to-all-start.3
  517.9 35.7 %reduce-scatter.7.cloned.1.call-done = bf16[1,1792,256]{2,1,0:T(8,128)(2,1)} async-done(((bf16[1,7168,256]{2,1,0:T(8,128)(2,1)}), bf16[1,1792,256]{2,1,0:T(8,128)(2,1)}) %reduce-scatter.7.cloned.1.call-update) | async-done | bytes 917520 | tf_op jit(solution)/shard_map/reduce_scatter | solution.py:127
  556.2 42.0 %reduce-scatter.9.cloned.1.call-done = bf16[1,1792,256]{2,1,0:T(8,128)(2,1)} async-done(((bf16[1,7168,256]{2,1,0:T(8,128)(2,1)}), bf16[1,1792,256]{2,1,0:T(8,128)(2,1)}) %reduce-scatter.9.cloned.1.call-update) | async-done | bytes 917520 | tf_op jit(solution)/shard_map/reduce_scatter | solution.py:130
  600.8 42.0 %reduce-scatter.11.cloned.1.call-done = bf16[1,1792,256]{2,1,0:T(8,128)(2,1)} async-done(((bf16[1,7168,256]{2,1,0:T(8,128)(2,1)}), bf16[1,1792,256]{2,1,0:T(8,128)(2,1)}) %reduce-scatter.11.cloned.1.call-update) | async-done | bytes 917520 | tf_op jit(solution)/shard_map/reduce_scatter | solution.py:133
  648.0 4.7 gather_fusion.3
  652.7 3.0 reshape.298
  655.7 3.7 reduce_sum.33
  (77 shorter events, 39.9 us)
Async XLA Ops:
  7.2 20.8 %copy-start = (bf16[192,7168]{1,0:T(8,128)(2,1)S(1)}, bf16[192,7168]{1,0:T(8,128)(2,1)}, u32[]{:S(2)}) copy-start(bf16[192,7168]{1,0:T(8,128)(2,1)} %param.8) | copy-start | bytes 8257540
  19.3 42.2 %all-to-all-start = ((bf16[16,1,32]{2,1,0:T(2,128)(2,1)}), bf16[16,1,32]{2,1,0:T(2,128)(2,1)S(1)}, u32[]{:S(2)}, u32[]{:S(2)}) async-start(bf16[16,1,32]{2,1,0:T(2,128)(2,1)} %all_to_all.25), calls=%async_computation | async-start | bytes 16384 | tf_op jit(solution)/shard_map/all_to_all | solution.py:59
  61.5 132.4 %all-to-all-start.2 = ((bf16[16,32,7168]{2,1,0:T(8,128)(2,1)}), bf16[16,32,7168]{2,1,0:T(8,128)(2,1)}, u32[]{:S(2)}, u32[]{:S(2)}) async-start(bf16[16,32,7168]{2,1,0:T(8,128)(2,1)} %get-tuple-element.26), calls=%async_computation.2 | async-start | bytes 14680064 | tf_op jit(solution)/shard_map/all_to_all | solution.py:57
  68.2 301.4 %all-gather.3.cloned.1.call-start = ((), (), s32[]{:S(2)}) async-start(), calls=%async_computation.9 | async-start | bytes 4587520 | tf_op jit(solution)/shard_map/all_gather | solution.py:77
  193.9 5.6 copy-start.3
  193.9 188.2 %all-to-all-start.1 = ((bf16[16,32,7168]{2,1,0:T(8,128)(2,1)}), bf16[16,32,7168]{2,1,0:T(8,128)(2,1)}, u32[]{:S(2)}, u32[]{:S(2)}) async-start(bf16[16,32,7168]{2,1,0:T(8,128)(2,1)} %get-tuple-element.25), calls=%async_computation.1 | async-start | bytes 14680064 | tf_op jit(solution)/shard_map/all_to_all | solution.py:58
  198.7 177.1 %all-gather.5.cloned.1.call-start = ((), (), s32[]{:S(2)}) async-start(), calls=%async_computation.10 | async-start | bytes 4587520 | tf_op jit(solution)/shard_map/all_gather | solution.py:76
  199.5 302.3 %reduce-scatter.13.cloned.1.call-start = ((), (), s32[]{:S(2)}) async-start(), calls=%async_computation.14 | async-start | bytes 8257536
  199.5 130.5 %collective-permute-start = (bf16[1,1792,256]{2,1,0:T(8,128)(2,1)S(1)}, bf16[1,1792,256]{2,1,0:T(8,128)(2,1)S(1)}, u32[]{:S(2)}, u32[]{:S(2)}) collective-permute-start(bf16[1,1792,256]{2,1,0:T(8,128)(2,1)S(1)} %copy-done.3), channel_id=1, source_target_pairs={{0,8},{8,16},{16,24},{24,0},{1,9},{9,17},{17,25},{25,1},{2,10},{10... | collective-permute-start | bytes 2752520 | tf_op jit(solution)/shard_map/ppermute | solution.py:13
  330.0 29.2 %collective-permute-start.1 = (bf16[1,1792,256]{2,1,0:T(8,128)(2,1)S(1)}, bf16[1,1792,256]{2,1,0:T(8,128)(2,1)}, u32[]{:S(2)}, u32[]{:S(2)}) collective-permute-start(bf16[1,1792,256]{2,1,0:T(8,128)(2,1)S(1)} %collective-permute-done), channel_id=1, source_target_pairs={{0,8},{8,16},{16,24},{24,0},{1,9},{9,17},{17,25},{25,1},{2,10},{10... | collective-permute-start | bytes 2752520 | tf_op jit(solution)/shard_map/ppermute | solution.py:13
  334.2 29.2 %collective-permute-start.2 = (bf16[1,1792,256]{2,1,0:T(8,128)(2,1)S(1)}, bf16[1,1792,256]{2,1,0:T(8,128)(2,1)S(1)}, u32[]{:S(2)}, u32[]{:S(2)}) collective-permute-start(bf16[1,1792,256]{2,1,0:T(8,128)(2,1)S(1)} %copy-done.3), channel_id=1, source_target_pairs={{0,24},{8,0},{16,8},{24,16},{1,25},{9,1},{17,9},{25,17},{2,26},{10... | collective-permute-start | bytes 2752520 | tf_op jit(solution)/shard_map/ppermute | solution.py:15
  382.1 6.6 copy-start.4
  388.7 7.4 %copy-start.2 = (bf16[1,7168,256]{2,1,0:T(8,128)(2,1)S(1)}, bf16[1,7168,256]{2,1,0:T(8,128)(2,1)}, u32[]{:S(2)}) copy-start(bf16[1,7168,256]{2,1,0:T(8,128)(2,1)} %all-gather.3.cloned.1.call-done) | copy-start | bytes 11010052
  448.5 105.2 %reduce-scatter.7.cloned.1.call-start = ((), (), s32[]{:S(2)}) async-start(), calls=%async_computation.11 | async-start | bytes 4587520 | tf_op jit(solution)/shard_map/reduce_scatter | solution.py:127
  455.6 142.7 %reduce-scatter.9.cloned.1.call-start = ((), (), s32[]{:S(2)}) async-start(), calls=%async_computation.12 | async-start | bytes 4587520 | tf_op jit(solution)/shard_map/reduce_scatter | solution.py:130
  462.7 180.1 %reduce-scatter.11.cloned.1.call-start = ((), (), s32[]{:S(2)}) async-start(), calls=%async_computation.13 | async-start | bytes 4587520 | tf_op jit(solution)/shard_map/reduce_scatter | solution.py:133
  497.2 10.9 %all-to-all-start.4 = ((bf16[16,1,32]{2,1,0:T(2,128)(2,1)}), bf16[16,1,32]{2,1,0:T(2,128)(2,1)S(1)}, u32[]{:S(2)}, u32[]{:S(2)}) async-start(bf16[16,1,32]{2,1,0:T(2,128)(2,1)} %convert_element_type.144), calls=%async_computation.4 | async-start | bytes 16384 | tf_op jit(solution)/shard_map/all_to_all | solution.py:112
  508.1 137.2 %all-to-all-start.3 = ((bf16[16,32,896]{2,1,0:T(8,128)(2,1)}), bf16[16,32,896]{2,1,0:T(8,128)(2,1)}, u32[]{:S(2)}, u32[]{:S(2)}) async-start(bf16[16,32,896]{2,1,0:T(8,128)(2,1)} %bitcast.9), calls=%async_computation.3 | async-start | bytes 1835008 | tf_op jit(solution)/shard_map/all_to_all | solution.py:105
  645.3 14.1 %copy-start.1 = (bf16[192,7168]{1,0:T(8,128)(2,1)S(1)}, bf16[192,7168]{1,0:T(8,128)(2,1)}, u32[]{:S(2)}) copy-start(bf16[192,7168]{1,0:T(8,128)(2,1)} %param.8) | copy-start | bytes 8257540
Sparse Core Ops, SparseCore 0:
  70.7 91.2 all-gather.2
  201.2 91.1 all-gather.4
  448.6 50.1 reduce-scatter.12
  501.1 52.5 reduce-scatter.6
  555.9 42.2 reduce-scatter.8
  600.5 42.2 reduce-scatter.10
